TPU v7x, 32 devices: a whole 2x2x4 slice. The times are simulated.
32 devices in a mesh: grp: 2 (over y), pool: 8 (over z, core), tp: 2 (over x).
Axes of the slice: x: 2, y: 2, z: 4, core: 2. Of those that a mesh axis runs over, the one named last changes fastest.
Arguments:
- home_query: bfloat16 [64, 8192], P(('grp', 'pool'), 'tp'), parts along dimension 0, may hold values from -12 to 12
- home_key: bfloat16 [64, 1024], P(('grp', 'pool'), 'tp'), parts along dimension 0, may hold values from -5 to 5
- home_value: bfloat16 [64, 1024], P(('grp', 'pool'), 'tp'), parts along dimension 0, may hold values from -5 to 5
- cache_keys: bfloat16 [8192, 1024], P(('grp', 'pool'), 'tp'), parts along dimension 0, may hold values from -12 to 12
- cache_values: bfloat16 [8192, 1024], P(('grp', 'pool'), 'tp'), parts along dimension 0, may hold values from -5 to 5
- cache_start: int32 [64], P('grp'), parts along dimension 0, may hold values from 0 to 4088, as said below
- cache_len: int32 [64], P('grp'), parts along dimension 0, may hold values from 8 to 64, as said below
- prompt_query: bfloat16 [7168, 8192], P(('grp', 'pool'), 'tp'), parts along dimension 0, may hold values from -12 to 12
- prompt_key: bfloat16 [7168, 1024], P(('grp', 'pool'), 'tp'), parts along dimension 0, may hold values from -12 to 12
- prompt_value: bfloat16 [7168, 1024], P(('grp', 'pool'), 'tp'), parts along dimension 0, may hold values from -5 to 5
- doc_ids: int32 [16, 448], P(('grp', 'pool')), parts along dimension 0, may hold values from 0 to 3, never falling along the last dimension, each value on 1 to 224 neighbouring positions
- out_weight: bfloat16 [8192, 8192], P('tp', 'pool'), may hold values from -0.0625 to 0.0625
Outputs:
- prompt_out: bfloat16 [7168, 8192], P(('grp', 'pool'), 'tp'), parts along dimension 0
- decode_out: bfloat16 [64, 8192], P(('grp', 'tp'), 'pool'), parts along dimension 0
There are 2 independent parts, one for each index of `grp`. A program takes and returns all parts, laid end to end along the dimension named above; an argument that names none is the same for every part. Nothing has to cross between parts.
Inputs may be any that keep to these rules, and one draw needn't show every extreme that they name: Each request's cache occupies cache_len rows from cache_start on, inside the 512 rows of one pool index and apart from every other request's rows; a pool index holds the caches of at most 8 requests, and some pool index of exactly 8. `cache_len`: some request has exactly 64 rows.
All inputs are finite; a program needn't handle non-finite values.
Results may differ from a plain program's by a relative error of at most 0.008.
Values may be sent and summed in bfloat16 or wider, within the bound.
A program may use at most 128 MiB of HBM per device.

v0:
```python
import jax
import jax.numpy as jnp
from jax import lax
from jax.sharding import PartitionSpec as P

HEAD_DIM = 128


def prompt_attention(
    prompt_query, prompt_key, prompt_value, doc_ids, kv_local, group_size, score_scale
):
    row_count = prompt_query.shape[0]
    doc_row = doc_ids[0]
    positions = jnp.arange(row_count, dtype=jnp.int32)
    allowed = (positions[:, None] >= positions[None, :]) & (doc_row[:, None] == doc_row[None, :])
    outputs = []
    for head_group in range(kv_local):
        width = group_size * HEAD_DIM
        query_heads = prompt_query[:, head_group * width : (head_group + 1) * width].reshape(
            row_count, group_size, HEAD_DIM
        )
        key_head = prompt_key[:, head_group * HEAD_DIM : (head_group + 1) * HEAD_DIM]
        value_head = prompt_value[:, head_group * HEAD_DIM : (head_group + 1) * HEAD_DIM]
        scores = (
            jnp.einsum("igd,jd->gij", query_heads, key_head, preferred_element_type=jnp.float32)
            * score_scale
        )
        scores = jnp.where(allowed[None], scores, -jnp.inf)
        highest = jnp.max(scores, axis=-1, keepdims=True)
        weights = jnp.exp(scores - highest)
        probabilities = (weights / jnp.sum(weights, axis=-1, keepdims=True)).astype(jnp.bfloat16)
        result = jnp.einsum(
            "gij,jd->igd", probabilities, value_head, preferred_element_type=jnp.float32
        )
        outputs.append(result.astype(jnp.bfloat16).reshape(row_count, width))
    return jnp.concatenate(outputs, axis=1)


def local(
    home_query,
    home_key,
    home_value,
    cache_keys,
    cache_values,
    cache_start,
    cache_len,
    prompt_query,
    prompt_key,
    prompt_value,
    doc_ids,
    out_weight,
):
    local_heads = home_query.shape[1] // HEAD_DIM
    kv_local = home_key.shape[1] // HEAD_DIM
    group_size = local_heads // kv_local
    score_scale = HEAD_DIM ** (-0.5)
    slot_total = 2 * home_query.shape[0]
    cap_rows = cache_keys.shape[0]
    request_total = cache_start.shape[0]
    all_query, all_key, all_value = (
        lax.all_gather(home_query, "pool", axis=0, tiled=True),
        lax.all_gather(home_key, "pool", axis=0, tiled=True),
        lax.all_gather(home_value, "pool", axis=0, tiled=True),
    )
    prompt_out = prompt_attention(
        prompt_query, prompt_key, prompt_value, doc_ids, kv_local, group_size, score_scale
    )
    my_index = lax.axis_index("pool")
    owner_of = cache_start // cap_rows
    request_index = jnp.arange(request_total, dtype=jnp.int32)
    same_owner = owner_of[:, None] == owner_of[None, :]
    earlier = request_index[None, :] < request_index[:, None]
    owner_rank = jnp.sum(same_owner & earlier, axis=1)
    is_mine = owner_of == my_index
    slot_ids = jnp.arange(slot_total, dtype=jnp.int32)
    selection = is_mine[None, :] & (owner_rank[None, :] == slot_ids[:, None])
    selection_bf = selection.astype(jnp.bfloat16)
    slot_query = jnp.dot(selection_bf, all_query, preferred_element_type=jnp.float32).astype(
        jnp.bfloat16
    )
    slot_key = jnp.dot(selection_bf, all_key, preferred_element_type=jnp.float32).astype(
        jnp.bfloat16
    )
    slot_value = jnp.dot(selection_bf, all_value, preferred_element_type=jnp.float32).astype(
        jnp.bfloat16
    )
    slot_first = jnp.sum(
        jnp.where(selection, (cache_start - my_index * cap_rows)[None, :], 0), axis=1
    )
    slot_length = jnp.sum(jnp.where(selection, cache_len[None, :], 0), axis=1)
    positions = jnp.arange(cap_rows, dtype=jnp.int32)
    in_segment = (positions[None, :] >= slot_first[:, None]) & (
        positions[None, :] < (slot_first + slot_length)[:, None]
    )
    query_heads = slot_query.reshape(slot_total, kv_local, group_size, HEAD_DIM)
    key_heads = cache_keys.reshape(cap_rows, kv_local, HEAD_DIM)
    value_heads = cache_values.reshape(cap_rows, kv_local, HEAD_DIM)
    scores = (
        jnp.einsum("mkgd,ckd->mkgc", query_heads, key_heads, preferred_element_type=jnp.float32)
        * score_scale
    )
    scores = jnp.where(in_segment[:, None, None, :], scores, -jnp.inf)
    own_score = (
        jnp.einsum(
            "mkgd,mkd->mkg",
            query_heads,
            slot_key.reshape(slot_total, kv_local, HEAD_DIM),
            preferred_element_type=jnp.float32,
        )
        * score_scale
    )
    highest = jnp.maximum(jnp.max(scores, axis=-1), own_score)
    cache_weights = jnp.exp(scores - highest[..., None])
    own_weight = jnp.exp(own_score - highest)
    denominator = jnp.sum(cache_weights, axis=-1) + own_weight
    cache_probs = (cache_weights / denominator[..., None]).astype(jnp.bfloat16)
    own_prob = (own_weight / denominator).astype(jnp.bfloat16)
    result = jnp.einsum(
        "mkgc,ckd->mkgd", cache_probs, value_heads, preferred_element_type=jnp.float32
    )
    result = result + own_prob.astype(jnp.float32)[..., None] * slot_value.reshape(
        slot_total, kv_local, 1, HEAD_DIM
    ).astype(jnp.float32)
    slot_out = result.astype(jnp.bfloat16).reshape(slot_total, local_heads * HEAD_DIM)
    pooled = lax.all_gather(slot_out, "pool", axis=0, tiled=True)
    assembled = jnp.take(pooled, owner_of * slot_total + owner_rank, axis=0)
    decode_out = lax.psum_scatter(
        jnp.dot(assembled, out_weight, preferred_element_type=jnp.float32),
        "tp",
        scatter_dimension=0,
        tiled=True,
    ).astype(jnp.bfloat16)
    return (prompt_out, decode_out)


def solution(mesh):
    return jax.shard_map(
        local,
        mesh=mesh,
        in_specs=(
            P(("grp", "pool"), "tp"),
            P(("grp", "pool"), "tp"),
            P(("grp", "pool"), "tp"),
            P(("grp", "pool"), "tp"),
            P(("grp", "pool"), "tp"),
            P("grp"),
            P("grp"),
            P(("grp", "pool"), "tp"),
            P(("grp", "pool"), "tp"),
            P(("grp", "pool"), "tp"),
            P(("grp", "pool"), None),
            P("tp", "pool"),
        ),
        out_specs=(P(("grp", "pool"), "tp"), P(("grp", "tp"), "pool")),
        check_vma=False,
    )
```

profile of v0, /device:TPU:0, one launch (start us, length us, event | category | flops | bytes accessed | tf_op | source)
XLA Modules:
  0.0 125.6 jit_solution(7688036058401376417)
XLA Ops:
  7.2 0.0 reduce-scatter.2.cloned.1.call-start
  7.2 0.7 broadcast_compare_fusion
  7.9 0.2 convert_reduce_fusion
  8.1 0.7 broadcast_subtract_fusion
  8.7 0.8 select_reduce_fusion
  9.5 0.1 fusion.82
  9.6 16.1 %all-gather = bf16[8,4,4096]{2,1,0:T(4,128)(2,1)S(1)} all-gather(bf16[1,4,4096]{2,1,0:T(4,128)(2,1)} %bitcast.165), channel_id=1, replica_groups=mesh['grp'=2,'pool'=8,'tp'=2] {'pool'}, dimensions={0}, use_global_device_ids=true | all-gather | bytes 294912 | tf_op jit(solution)/shard_map/all_gather | solution.py:61
  25.7 0.1 reshape.182
  25.8 0.1 convolution_convert_fusion
  26.0 1.2 reshape.167
  27.1 14.2 %all-gather.1 = bf16[8,4,512]{2,1,0:T(4,128)(2,1)S(1)} all-gather(bf16[1,4,512]{2,1,0:T(4,128)(2,1)} %bitcast.167), channel_id=1, replica_groups=mesh['grp'=2,'pool'=8,'tp'=2] {'pool'}, dimensions={0}, use_global_device_ids=true | all-gather | bytes 36864 | tf_op jit(solution)/shard_map/all_gather | solution.py:62
  41.4 0.1 fusion.36
  41.5 0.2 fusion.78
  41.7 0.4 fusion.109
  42.1 0.2 fusion.54
  42.3 14.2 %all-gather.2 = bf16[8,4,512]{2,1,0:T(4,128)(2,1)S(1)} all-gather(bf16[1,4,512]{2,1,0:T(4,128)(2,1)} %bitcast.168), channel_id=1, replica_groups=mesh['grp'=2,'pool'=8,'tp'=2] {'pool'}, dimensions={0}, use_global_device_ids=true | all-gather | bytes 36864 | tf_op jit(solution)/shard_map/all_gather | solution.py:63
  56.6 0.1 fusion.38
  56.7 1.2 reshape.169
  57.9 0.3 fusion.35
  58.2 14.8 %all_gather.15 = bf16[64,4096]{1,0:T(8,128)(2,1)S(1)} all-gather(bf16[8,4096]{1,0:T(8,128)(2,1)S(1)} %bitcast.163), channel_id=1, replica_groups=mesh['grp'=2,'pool'=8,'tp'=2] {'pool'}, dimensions={0}, use_global_device_ids=true | all-gather | bytes 589824 | tf_op jit(solution)/shard_map/all_gather | solution.py:125
  73.1 0.7 gather_fusion
  73.8 0.0 copy-start.1
  73.8 0.0 copy-start
  73.8 5.7 %fusion.55 = f32[32,1024]{1,0:T(8,128)} fusion(bf16[4096,1024]{1,0:T(8,128)(2,1)} %param.23, bf16[32,4096]{1,0:T(8,128)(2,1)S(1)} %gather_fusion, pred[32]{0:T(512)(128)(4,1)S(1)} %get-tuple-element.4), kind=kOutput, calls=%fused_computation.85 | convolution fusion | flops 268566528 | bytes 8781856 | tf_op jit(solution)/shard_map/dot_general | solution.py:128
  79.5 0.0 reduce-scatter.2.cloned.1.call-update
  79.5 2.8 %slice_bitcast_fusion.3 = (bf16[56,8,8,128]{3,2,1,0:T(8,128)(2,1)S(1)}, bf16[56,8,8,128]{3,2,1,0:T(8,128)(2,1)S(1)}, bf16[56,8,8,128]{3,2,1,0:T(8,128)(2,1)S(1)}, bf16[56,8,8,128]{3,2,1,0:T(8,128)(2,1)S(1)}) fusion(bf16[448,4096]{1,0:T(8,128)(2,1)} %param.19), kind=kLoop, calls=%fused_computation.77 | loop fusion | bytes 7340032
  82.4 0.2 fusion.51
  82.6 1.1 fusion.48
  83.7 1.1 fusion.45
  84.9 4.9 %fusion.108 = (f32[8,448]{1,0:T(8,128)S(1)}, f32[8,448,448]{1,2,0:T(8,128)}) fusion(f32[448,448,8]{1,0,2:T(8,128)S(1)} %fusion.48, pred[448,448]{0,1:T(8,128)(4,1)S(1)} %fusion.51), kind=kOutput, calls=%fused_computation.156 | output fusion | flops 9634239 | bytes 13060096 | tf_op jit(solution)/shard_map/sub | solution.py:30
  89.8 4.7 %fusion.107 = (f32[8,448]{1,0:T(8,128)S(1)}, f32[8,448,448]{1,2,0:T(8,128)}) fusion(f32[448,448,8]{1,0,2:T(8,128)S(1)} %fusion.45, pred[448,448]{0,1:T(8,128)(4,1)S(1)} %fusion.51), kind=kOutput, calls=%fused_computation.155 | output fusion | flops 9634239 | bytes 13060096 | tf_op jit(solution)/shard_map/sub | solution.py:30
  94.5 1.1 fusion.42
  95.6 3.0 %fusion.106 = (f32[8,448]{1,0:T(8,128)S(1)}, f32[8,448,448]{1,2,0:T(8,128)S(1)}) fusion(f32[448,448,8]{1,0,2:T(8,128)S(1)} %fusion.42, pred[448,448]{0,1:T(8,128)(4,1)S(1)} %fusion.51), kind=kOutput, calls=%fused_computation.154 | output fusion | flops 9634239 | bytes 13060096 | tf_op jit(solution)/shard_map/sub | solution.py:30
  98.7 1.1 fusion.39
  99.8 0.0 copy-start.2
  99.8 0.0 slice-start
  99.8 4.8 %fusion.105 = (f32[8,448]{1,0:T(8,128)S(1)}, f32[8,448,448]{1,2,0:T(8,128)}) fusion(f32[448,448,8]{1,0,2:T(8,128)S(1)} %fusion.39, pred[448,448]{0,1:T(8,128)(4,1)S(1)} %fusion.51), kind=kOutput, calls=%fused_computation.153 | output fusion | flops 9634239 | bytes 13060096 | tf_op jit(solution)/shard_map/sub | solution.py:30
  104.6 4.5 %fusion.28 = bf16[8,56,8,128]{3,2,1,0:T(8,128)(2,1)S(1)} fusion(f32[8,448,448]{1,2,0:T(8,128)} %get-tuple-element.21, f32[8,448]{1,0:T(8,128)S(1)} %get-tuple-element.20, bf16[448,512]{1,0:T(8,128)(2,1)S(1)} %copy-done.2), kind=kOutput, calls=%fused_computation.43 | convolution fusion | flops 414711808 | bytes 7471104 | tf_op jit(solution)/shard_map/gij,jd->igd/dot_general | solution.py:32
  109.2 1.3 %fusion.29 = bf16[8,56,8,128]{3,2,1,0:T(8,128)(2,1)S(1)} fusion(f32[8,448,448]{1,2,0:T(8,128)S(1)} %bitcast.170, f32[8,448]{1,0:T(8,128)S(1)} %get-tuple-element.18, bf16[448,512]{1,0:T(8,128)(2,1)S(1)} %copy-done.2), kind=kOutput, calls=%fused_computation.44 | convolution fusion | flops 414711808 | bytes 8388608 | tf_op jit(solution)/shard_map/gij,jd->igd/dot_general | solution.py:32
  110.5 0.3 copy_bitcast_fusion.2
  110.8 0.0 slice-start.3
  110.8 1.3 %fusion.30 = bf16[8,56,8,128]{3,2,1,0:T(8,128)(2,1)S(1)} fusion(f32[8,448,448]{1,2,0:T(8,128)S(1)} %get-tuple-element.17, f32[8,448]{1,0:T(8,128)S(1)} %get-tuple-element.16, bf16[448,512]{1,0:T(8,128)(2,1)S(1)} %copy-done.2), kind=kOutput, calls=%fused_computation.45 | convolution fusion | flops 414711808 | bytes 8388608 | tf_op jit(solution)/shard_map/gij,jd->igd/dot_general | solution.py:32
  112.1 0.6 slice-done.2
  112.7 1.1 slice-done.3
  113.7 1.3 %fusion.31 = bf16[8,56,8,128]{3,2,1,0:T(8,128)(2,1)S(1)} fusion(f32[8,448,448]{1,2,0:T(8,128)S(1)} %bitcast.172, f32[8,448]{1,0:T(8,128)S(1)} %get-tuple-element.14, bf16[448,512]{1,0:T(8,128)(2,1)S(1)} %copy-done.2), kind=kOutput, calls=%fused_computation.46 | convolution fusion | flops 414711808 | bytes 8388608 | tf_op jit(solution)/shard_map/gij,jd->igd/dot_general | solution.py:32
  115.0 0.3 copy_bitcast_fusion
  115.3 2.0 %pad_maximum_fusion = bf16[448,4096]{1,0:T(8,128)(2,1)} fusion(bf16[448,1024]{1,0:T(8,128)(2,1)S(1)} %get-tuple-element.24, bf16[448,1024]{1,0:T(8,128)(2,1)S(1)} %get-tuple-element.25, bf16[448,1024]{1,0:T(8,128)(2,1)S(1)} %get-tuple-element.26, bf16[448,1024]{1,0:T(8,128)(2,1)S(1)} %get-tuple-element.27), kind=kLoop, calls=%fused_computation.22 | loop fusion | flops 14680064 | bytes 7340032 | tf_op jit(solution)/shard_map/concatenate | solution.py:36
  117.3 1.5 %convert_element_type.97 = bf16[16,1024]{1,0:T(8,128)(2,1)} convert(f32[16,1024]{1,0:T(8,128)} %reduce-scatter.2.cloned.1.call-done) | non-fusion elementwise | flops 16384 | bytes 98304 | tf_op jit(solution)/shard_map/convert_element_type | solution.py:132
  (19 shorter events, 0.1 us)
Async XLA Ops:
  7.2 110.1 %reduce-scatter.2.cloned.1.call-start = ((), (), s32[]{:S(2)}) async-start(), calls=%async_computation.1 | async-start | bytes 196608 | tf_op jit(solution)/shard_map/reduce_scatter | solution.py:127
  73.8 8.6 %copy-start.1 = (s32[1,448]{1,0:T(1,128)S(1)}, s32[1,448]{1,0:T(1,128)}, u32[]{:S(2)}) copy-start(s32[1,448]{1,0:T(1,128)} %param.22) | copy-start | bytes 5380
  73.8 8.8 %copy-start = (bf16[448,512]{1,0:T(8,128)(2,1)S(1)}, bf16[448,512]{1,0:T(8,128)(2,1)}, u32[]{:S(2)}) copy-start(bf16[448,512]{1,0:T(8,128)(2,1)} %param.20) | copy-start | bytes 1376260
  99.8 4.8 %copy-start.2 = (bf16[448,512]{1,0:T(8,128)(2,1)S(1)}, bf16[448,512]{1,0:T(8,128)(2,1)}, u32[]{:S(2)}) copy-start(bf16[448,512]{1,0:T(8,128)(2,1)} %param.21) | copy-start | bytes 1376260
  99.8 9.3 %slice-start = ((s8[7340032]{0:T(1024)(128)(4,1)}), s8[4194304]{0:T(1024)(128)(4,1)S(1)}, s32[]{:S(2)}) async-start(s8[7340032]{0:T(1024)(128)(4,1)} %bitcast.169), calls=%async_computation.2 | async-start | bytes 8388608
  104.6 4.5 %slice-start.1 = ((s8[7340032]{0:T(1024)(128)(4,1)}), s8[3145728]{0:T(1024)(128)(4,1)S(1)}, s32[]{:S(2)}) async-start(s8[7340032]{0:T(1024)(128)(4,1)} %bitcast.169), calls=%async_computation.3 | async-start | bytes 6291456
  110.5 2.2 %slice-start.2 = ((s8[7340032]{0:T(1024)(128)(4,1)}), s8[4194304]{0:T(1024)(128)(4,1)S(1)}, s32[]{:S(2)}) async-start(s8[7340032]{0:T(1024)(128)(4,1)} %bitcast.171), calls=%async_computation.4 | async-start | bytes 8388608
  110.8 3.0 %slice-start.3 = ((s8[7340032]{0:T(1024)(128)(4,1)}), s8[3145728]{0:T(1024)(128)(4,1)S(1)}, s32[]{:S(2)}) async-start(s8[7340032]{0:T(1024)(128)(4,1)} %bitcast.171), calls=%async_computation.5 | async-start | bytes 6291456
Sparse Core Ops, SparseCore 0:
  79.7 11.5 reduce-scatter.1
where the time goes:
time: 126 us
  blocking collectives  59.4 us (47%)
  other arithmetic  23.8 us (19%)
  matrix products  19.8 us (16%)
  between operations  14.3 us (11%)
  local copies, waits for them, and re-layouts  8.22 us (7%)
    sub x4, other arithmetic, prompt_attention(): weights = jnp.exp(scores - highest)  17.5 us
    all_gather x1, blocking collectives, local(): lax.all_gather(home_query, 'pool', axis=0, tiled=True)  16.1 us
    all_gather x1, blocking collectives, local(): pooled = lax.all_gather(slot_out, 'pool', axis=0, tiled=True)  14.8 us
    all_gather x1, blocking collectives, local(): lax.all_gather(home_key, 'pool', axis=0, tiled=True)  14.2 us
    all_gather x1, blocking collectives, local(): lax.all_gather(home_value, 'pool', axis=0, tiled=True)  14.2 us
    dot_general x4, matrix products, prompt_attention(): jnp.einsum('gij,jd->igd', probabilities, value_head, preferred_element_ty...  8.37 us
    dot_general x1, matrix products, local(): jnp.dot(assembled, out_weight, preferred_element_type=jnp.float32)  5.69 us
    unnamed x19, local copies, waits for them, and re-layouts  4.64 us
  transfers between devices with their start and end apart: 1, of which 0 were waited for; matrix products, arithmetic and copies ran while one was open for 29% of the time, Pallas kernels for 0%

commit v1 on v0

v1 whole, which is shorter than its diff:
```python
import functools
import math

import jax
import jax.numpy as jnp
from jax import lax
from jax.experimental import pallas as pl
from jax.experimental.pallas import tpu as pltpu
from jax.sharding import PartitionSpec as P

HEAD_DIM = 128
LANES = 128
ROW_BLOCK = 32
MASKED = -1e30
SCALE = HEAD_DIM ** (-0.5)
F32 = jnp.float32
BF16 = jnp.bfloat16
MESH = pl.DeviceIdType.MESH
NT = (((1,), (1,)), ((), ()))


def windows(rows):
    width = -(-(rows // 2 + ROW_BLOCK) // LANES) * LANES
    out = []
    for first in range(0, rows, ROW_BLOCK):
        end = first + ROW_BLOCK
        low = max(0, end - width)
        high = min(rows, max(end, low + -(-(end - low) // LANES) * LANES))
        out.append((first, low, high))
    return width, out


def fill_bias(doc_ref, bias_ref):
    rows = doc_ref.shape[1]
    for first, low, high in windows(rows)[1]:
        span = high - low
        row_at = first + lax.broadcasted_iota(jnp.int32, (ROW_BLOCK, span), 0)
        col_at = low + lax.broadcasted_iota(jnp.int32, (ROW_BLOCK, span), 1)
        doc = jnp.broadcast_to(doc_ref[:, low:high], (ROW_BLOCK, span)).astype(F32)
        own = jnp.sum(jnp.where(row_at == col_at, doc, 0.0), axis=1, keepdims=True)
        allowed = (col_at <= row_at) & (doc == own)
        bias_ref[first : first + ROW_BLOCK, :span] = jnp.where(allowed, 0.0, MASKED)


def prompt_group(query, key, value, bias_ref, wide_ref, out, group_size):
    rows = key.shape[0]
    wide_ref[:, :HEAD_DIM] = value[...]
    factor = SCALE * math.log2(math.e)
    for first, low, high in windows(rows)[1]:
        span = high - low
        block = slice(first, first + ROW_BLOCK)
        stacked = jnp.concatenate(
            [query[block, h * HEAD_DIM : (h + 1) * HEAD_DIM] for h in range(group_size)], axis=0
        )
        scores = lax.dot_general(stacked, key[low:high, :], NT, preferred_element_type=F32)
        scores = scores.reshape(group_size, ROW_BLOCK, span) + bias_ref[block, :span][None]
        highest = jnp.max(scores, axis=-1, keepdims=True)
        weights = jnp.exp2((scores - highest) * factor).astype(BF16)
        weights = weights.reshape(group_size * ROW_BLOCK, span)
        result = jnp.dot(weights, wide_ref[low:high, :], preferred_element_type=F32)
        result = (result[:, :HEAD_DIM] / result[:, HEAD_DIM:]).astype(BF16)
        for h in range(group_size):
            out[block, h * HEAD_DIM : (h + 1) * HEAD_DIM] = result[
                h * ROW_BLOCK : (h + 1) * ROW_BLOCK
            ]


def prompt_kernel(group_size, doc_ref, q_ref, k_ref, v_ref, o_ref, bias_ref, wide_ref):
    @pl.when(pl.program_id(0) == 0)
    def _():
        fill_bias(doc_ref, bias_ref)
        wide_ref[:, HEAD_DIM:] = jnp.ones((wide_ref.shape[0], HEAD_DIM), BF16)

    prompt_group(q_ref, k_ref, v_ref, bias_ref, wide_ref, o_ref, group_size)


def prompt_attention(prompt_query, prompt_key, prompt_value, doc_ids):
    rows = prompt_query.shape[0]
    kv_local = prompt_key.shape[1] // HEAD_DIM
    width = prompt_query.shape[1] // kv_local
    return pl.pallas_call(
        functools.partial(prompt_kernel, width // HEAD_DIM),
        grid=(kv_local,),
        out_shape=jax.ShapeDtypeStruct(prompt_query.shape, BF16),
        in_specs=[
            pl.BlockSpec((1, rows), lambda g: (0, 0)),
            pl.BlockSpec((rows, width), lambda g: (0, g)),
            pl.BlockSpec((rows, HEAD_DIM), lambda g: (0, g)),
            pl.BlockSpec((rows, HEAD_DIM), lambda g: (0, g)),
        ],
        out_specs=pl.BlockSpec((rows, width), lambda g: (0, g)),
        scratch_shapes=[
            pltpu.VMEM((rows, windows(rows)[0]), F32),
            pltpu.VMEM((rows, 2 * HEAD_DIM), BF16),
        ],
        compiler_params=pltpu.CompilerParams(vmem_limit_bytes=40 * 1024 * 1024),
    )(doc_ids, prompt_query, prompt_key, prompt_value)


def routing(start_row, len_row, me, cap_rows, n, slots):
    total = start_row.shape[1]
    owner = jnp.zeros_like(start_row)
    for p in range(1, n):
        owner = owner + (start_row >= p * cap_rows).astype(jnp.int32)
    owner = jnp.broadcast_to(owner, (total, total)).astype(F32)
    at_row = lax.broadcasted_iota(jnp.int32, (total, total), 0)
    at_col = lax.broadcasted_iota(jnp.int32, (total, total), 1)
    same = at_row == at_col
    owner_col = jnp.sum(jnp.where(same, owner, 0.0), axis=1, keepdims=True)
    together = owner == owner_col
    rank = jnp.sum(jnp.where(together & (at_row < at_col), 1.0, 0.0), axis=0, keepdims=True)
    rank_col = jnp.sum(jnp.where(together & (at_col < at_row), 1.0, 0.0), axis=1, keepdims=True)
    slot_at = lax.broadcasted_iota(jnp.int32, (slots, total), 0).astype(F32)
    mine = (owner[:1] == me.astype(F32)) & (rank == slot_at)
    first = jnp.sum(jnp.where(mine, start_row - me * cap_rows, 0), axis=1, keepdims=True)
    length = jnp.sum(jnp.where(mine, len_row, 0), axis=1, keepdims=True)
    place = lax.broadcasted_iota(jnp.int32, (total, n * slots), 1).astype(F32)
    unpack = jnp.where(owner_col * slots + rank_col == place, 1.0, 0.0).astype(BF16)
    return jnp.where(mine, 1.0, 0.0).astype(BF16), first, length, unpack


def slot_rows(select, gathered, flat):
    n, rows, width = gathered.shape
    for s in range(n):
        flat[s * rows : (s + 1) * rows, :width] = gathered[s].astype(F32)
    return jnp.dot(select, flat[:, :width].astype(BF16), preferred_element_type=F32)


def decode_kernel(
    n, tps, start_ref, len_ref, hq, hk, hv, ck_hbm, cv_hbm, w_hbm, out_ref,
    all_q, all_k, all_v, flat, ck, cv, w, pooled, part, part_in,
    load_sem, w_sem, send_sem, recv_sem, out_send, out_recv, tp_send, tp_recv,
):
    me, tpi = lax.axis_index("pool"), lax.axis_index("tp")
    slots = pooled.shape[1]
    cap_rows = ck.shape[0]
    kv_local = ck.shape[1] // HEAD_DIM
    group_size = hq.shape[1] // ck.shape[1]
    pieces = w_sem.shape[0]
    depth = w.shape[0] // pieces

    barrier = pltpu.get_barrier_semaphore()
    for d in range(1, n):
        pl.semaphore_signal(
            barrier, inc=1, device_id={"pool": lax.rem(me + d, n)}, device_id_type=MESH
        )
    for d in range(1, tps):
        pl.semaphore_signal(
            barrier, inc=1, device_id={"tp": lax.rem(tpi + d, tps)}, device_id_type=MESH
        )
    loads = [
        pltpu.make_async_copy(src, dst, load_sem.at[i])
        for i, (src, dst) in enumerate(
            [(hq, all_q.at[me]), (hk, all_k.at[me]), (hv, all_v.at[me]), (ck_hbm, ck), (cv_hbm, cv)]
        )
    ]
    for load in loads:
        load.start()
    w_loads = [
        pltpu.make_async_copy(
            w_hbm.at[i * depth : (i + 1) * depth], w.at[i * depth : (i + 1) * depth], w_sem.at[i]
        )
        for i in range(pieces)
    ]
    for load in w_loads:
        load.start()
    pl.semaphore_wait(barrier, n - 1 + tps - 1)
    sends = []
    for d in range(1, n):
        for i, (src, dst) in enumerate([(hq, all_q), (hk, all_k), (hv, all_v)]):
            sends.append(
                pltpu.make_async_remote_copy(
                    src_ref=src, dst_ref=dst.at[me],
                    send_sem=send_sem.at[i, d], recv_sem=recv_sem.at[i, d],
                    device_id={"pool": lax.rem(me + d, n)}, device_id_type=MESH,
                )
            )
            sends[-1].start()

    select, first, length, unpack = routing(start_ref[...], len_ref[...], me, cap_rows, n, slots)
    at = lax.broadcasted_iota(jnp.int32, (slots, cap_rows), 1)
    bias = jnp.where((at >= first) & (at < first + length), 0.0, MASKED)
    bias = jnp.concatenate([bias] * group_size, axis=0)

    for load in loads:
        load.wait()
    for send in sends:
        send.wait()
    slot_key = slot_rows(select, all_k, flat)
    slot_value = slot_rows(select, all_v, flat)
    slot_query = slot_rows(select, all_q, flat)
    for g in range(kv_local):
        lanes = slice(g * HEAD_DIM, (g + 1) * HEAD_DIM)
        base = g * group_size * HEAD_DIM
        query = jnp.concatenate(
            [
                slot_query[:, base + h * HEAD_DIM : base + (h + 1) * HEAD_DIM]
                for h in range(group_size)
            ],
            axis=0,
        )
        scores = (
            lax.dot_general(query.astype(BF16), ck[:, lanes], NT, preferred_element_type=F32)
            * SCALE
            + bias
        )
        own_key = jnp.concatenate([slot_key[:, lanes]] * group_size, axis=0)
        own_value = jnp.concatenate([slot_value[:, lanes]] * group_size, axis=0)
        own = jnp.sum(query * own_key, axis=1, keepdims=True) * SCALE
        highest = jnp.maximum(jnp.max(scores, axis=1, keepdims=True), own)
        weights = jnp.exp(scores - highest)
        own_weight = jnp.exp(own - highest)
        total = jnp.sum(weights, axis=1, keepdims=True) + own_weight
        probs = (weights / total).astype(BF16)
        own_prob = (own_weight / total).astype(BF16).astype(F32)
        result = jnp.dot(probs, cv[:, lanes], preferred_element_type=F32) + own_prob * own_value
        for h in range(group_size):
            pooled[me, :, base + h * HEAD_DIM : base + (h + 1) * HEAD_DIM] = result[
                h * slots : (h + 1) * slots
            ].astype(BF16)

    sends = []
    for d in range(1, n):
        sends.append(
            pltpu.make_async_remote_copy(
                src_ref=pooled.at[me], dst_ref=pooled.at[me],
                send_sem=out_send.at[d], recv_sem=out_recv.at[d],
                device_id={"pool": lax.rem(me + d, n)}, device_id_type=MESH,
            )
        )
        sends[-1].start()
    for load in w_loads:
        load.wait()
    for send in sends:
        send.wait()
    sums = None
    for i in range(pieces):
        span = slice(i * depth, (i + 1) * depth)
        joined = jnp.concatenate([pooled[s, :, span].astype(F32) for s in range(n)], axis=0)
        attended = jnp.dot(unpack, joined.astype(BF16), preferred_element_type=F32).astype(BF16)
        term = jnp.dot(attended, w[span, :], preferred_element_type=F32)
        sums = term if sums is None else sums + term
    rows = part.shape[1]
    for t in range(tps):
        part[t] = sums[t * rows : (t + 1) * rows]
    sends = []
    for d in range(1, tps):
        peer = lax.rem(tpi + d, tps)
        sends.append(
            pltpu.make_async_remote_copy(
                src_ref=part.at[peer], dst_ref=part_in.at[d],
                send_sem=tp_send.at[d], recv_sem=tp_recv.at[d],
                device_id={"tp": peer}, device_id_type=MESH,
            )
        )
        sends[-1].start()
    for send in sends:
        send.wait()
    total = part[tpi]
    for d in range(1, tps):
        total = total + part_in[d]
    out_ref[...] = total.astype(BF16)


def decode(
    n, tps, home_query, home_key, home_value, cache_keys, cache_values, start, length, out_weight
):
    requests = start.shape[0]
    home_rows, width = home_query.shape
    kv_width = home_key.shape[1]
    slots = 2 * home_rows
    out_rows, out_cols = requests // tps, out_weight.shape[1]
    pieces = 4
    vmem, hbm = pl.BlockSpec(memory_space=pltpu.VMEM), pl.BlockSpec(memory_space=pl.ANY)
    dma = pltpu.SemaphoreType.DMA
    return pl.pallas_call(
        functools.partial(decode_kernel, n, tps),
        out_shape=jax.ShapeDtypeStruct((out_rows, out_cols), BF16),
        in_specs=[vmem, vmem] + [hbm] * 6,
        out_specs=vmem,
        scratch_shapes=[
            pltpu.VMEM((n, home_rows, width), BF16),
            pltpu.VMEM((n, home_rows, kv_width), BF16),
            pltpu.VMEM((n, home_rows, kv_width), BF16),
            pltpu.VMEM((requests, width), F32),
            pltpu.VMEM(cache_keys.shape, BF16),
            pltpu.VMEM(cache_values.shape, BF16),
            pltpu.VMEM(out_weight.shape, BF16),
            pltpu.VMEM((n, slots, width), BF16),
            pltpu.VMEM((tps, out_rows, out_cols), F32),
            pltpu.VMEM((tps, out_rows, out_cols), F32),
            dma((5,)), dma((pieces,)), dma((3, n)), dma((3, n)),
            dma((n,)), dma((n,)), dma((tps,)), dma((tps,)),
        ],
        compiler_params=pltpu.CompilerParams(
            collective_id=0, has_side_effects=True, vmem_limit_bytes=40 * 1024 * 1024
        ),
    )(
        start.reshape(1, requests), length.reshape(1, requests),
        home_query, home_key, home_value, cache_keys, cache_values, out_weight,
    )


def solution(mesh):
    n, tps = mesh.shape["pool"], mesh.shape["tp"]

    def local(
        home_query, home_key, home_value, cache_keys, cache_values, cache_start, cache_len,
        prompt_query, prompt_key, prompt_value, doc_ids, out_weight,
    ):
        decode_out = decode(
            n, tps, home_query, home_key, home_value, cache_keys, cache_values,
            cache_start, cache_len, out_weight,
        )
        prompt_out = prompt_attention(prompt_query, prompt_key, prompt_value, doc_ids)
        return prompt_out, decode_out

    return jax.shard_map(
        local,
        mesh=mesh,
        in_specs=(
            P(("grp", "pool"), "tp"),
            P(("grp", "pool"), "tp"),
            P(("grp", "pool"), "tp"),
            P(("grp", "pool"), "tp"),
            P(("grp", "pool"), "tp"),
            P("grp"),
            P("grp"),
            P(("grp", "pool"), "tp"),
            P(("grp", "pool"), "tp"),
            P(("grp", "pool"), "tp"),
            P(("grp", "pool"), None),
            P("tp", "pool"),
        ),
        out_specs=(P(("grp", "pool"), "tp"), P(("grp", "tp"), "pool")),
        check_vma=False,
    )
```

time: 126 us -> 48.9 us (0.39)
  the two profiles are of different devices: /device:TPU:0 before, /device:TPU:29 now
where the time goes in v1:
time: 48.9 us; the launch traced here: 48.5 us
  Pallas kernels  38.3 us (78%)
  local copies, waits for them, and re-layouts  9.53 us (19%)
  between operations  0.7 us (1%)
    pallas_call x1, Pallas kernels, decode(): pl.pallas_call(functools.partial(decode_kernel, n, tps), out_shape=jax.Sh...  30.6 us
    unnamed x25, local copies, waits for them, and re-layouts  9.53 us
    pallas_call x1, Pallas kernels, prompt_attention(): pl.pallas_call(functools.partial(prompt_kernel, width // HEAD_DIM), grid=...  7.73 us

profile of v1, /device:TPU:29, one launch (start us, length us, event | category | flops | bytes accessed | tf_op | source)
XLA Modules:
  0.0 48.5 jit_solution(10023249113489223404)
XLA Ops:
  0.6 0.0 copy-start
  0.6 3.4 %copy-done = bf16[4096,1024]{1,0:T(8,128)(2,1)S(1)} copy-done((bf16[4096,1024]{1,0:T(8,128)(2,1)S(1)}, bf16[4096,1024]{1,0:T(8,128)(2,1)}, u32[]{:S(2)}) %copy-start) | copy-done | bytes 8388632
  4.0 0.0 copy-start.2
  4.0 1.0 %copy-done.2 = bf16[512,512]{1,0:T(8,128)(2,1)S(1)} copy-done((bf16[512,512]{1,0:T(8,128)(2,1)S(1)}, bf16[512,512]{1,0:T(8,128)(2,1)}, u32[]{:S(2)}) %copy-start.2) | copy-done | bytes 524312
  5.1 0.0 copy-start.3
  5.1 1.0 %copy-done.3 = bf16[512,512]{1,0:T(8,128)(2,1)S(1)} copy-done((bf16[512,512]{1,0:T(8,128)(2,1)S(1)}, bf16[512,512]{1,0:T(8,128)(2,1)}, u32[]{:S(2)}) %copy-start.3) | copy-done | bytes 524312
  6.1 0.0 copy-start.6
  6.1 0.8 %copy-done.6 = bf16[4,4096]{1,0:T(4,128)(2,1)S(1)} copy-done((bf16[4,4096]{1,0:T(4,128)(2,1)S(1)}, bf16[4,4096]{1,0:T(4,128)(2,1)}, u32[]{:S(2)}) %copy-start.6) | copy-done | bytes 32792
  6.9 0.0 copy-start.7
  6.9 0.7 %copy-done.7 = bf16[4,512]{1,0:T(4,128)(2,1)S(1)} copy-done((bf16[4,512]{1,0:T(4,128)(2,1)S(1)}, bf16[4,512]{1,0:T(4,128)(2,1)}, u32[]{:S(2)}) %copy-start.7) | copy-done | bytes 4120
  7.5 0.0 copy-start.8
  7.5 0.7 %copy-done.8 = bf16[4,512]{1,0:T(4,128)(2,1)S(1)} copy-done((bf16[4,512]{1,0:T(4,128)(2,1)S(1)}, bf16[4,512]{1,0:T(4,128)(2,1)}, u32[]{:S(2)}) %copy-start.8) | copy-done | bytes 4120
  8.2 0.0 copy-start.10
  8.2 0.7 %copy-done.10 = s32[32]{0:T(128)S(1)} copy-done((s32[32]{0:T(128)S(1)}, s32[32]{0:T(128)}, u32[]{:S(2)}) %copy-start.10) | copy-done | bytes 152
  8.9 0.0 copy-start.11
  8.9 0.7 %copy-done.11 = s32[32]{0:T(128)S(1)} copy-done((s32[32]{0:T(128)S(1)}, s32[32]{0:T(128)}, u32[]{:S(2)}) %copy-start.11) | copy-done | bytes 152
  9.5 0.0 copy-start.1
  9.5 0.0 copy-start.4
  9.6 0.0 copy-start.5
  9.6 0.0 copy-start.9
  9.6 30.6 %shard_map.132 = bf16[16,1024]{1,0:T(8,128)(2,1)S(1)} custom-call(s32[1,32]{1,0:T(1,128)S(1)} %bitcast.2, s32[1,32]{1,0:T(1,128)S(1)} %bitcast.3, bf16[4,4096]{1,0:T(4,128)(2,1)S(1)} %copy-done.6, bf16[4,512]{1,0:T(4,128)(2,1)S(1)} %copy-done.7, bf16[4,512]{1,0:T(4,128)(2,1)S(1)} %copy-done.8, bf16[512,512]{1,0:T(8,128)(2,1)S(1)} %copy-done.2, ...), custom_call_target="tpu_custom_call" | custom-call | tf_op jit(solution)/shard_map/pallas_call | solution.py:276
  40.1 0.0 copy-done.1
  40.2 0.0 copy-done.4
  40.2 0.0 copy-done.5
  40.2 0.0 copy-done.9
  40.2 7.7 %shard_map.131 = bf16[448,4096]{1,0:T(8,128)(2,1)} custom-call(s32[1,448]{1,0:T(1,128)S(1)} %copy-done.9, bf16[448,4096]{1,0:T(8,128)(2,1)S(1)} %copy-done.1, bf16[448,512]{1,0:T(8,128)(2,1)S(1)} %copy-done.4, bf16[448,512]{1,0:T(8,128)(2,1)S(1)} %copy-done.5), custom_call_target="tpu_custom_call" | custom-call | tf_op jit(solution)/shard_map/pallas_call | solution.py:81
  47.9 0.6 %copy.15 = bf16[16,1024]{1,0:T(8,128)(2,1)} copy(bf16[16,1024]{1,0:T(8,128)(2,1)S(1)} %shard_map.132) | data formatting | bytes 65536
Async XLA Ops:
  0.6 3.4 %copy-start = (bf16[4096,1024]{1,0:T(8,128)(2,1)S(1)}, bf16[4096,1024]{1,0:T(8,128)(2,1)}, u32[]{:S(2)}) copy-start(bf16[4096,1024]{1,0:T(8,128)(2,1)} %w_hbm.1) | copy-start | bytes 25165828
  4.0 1.0 %copy-start.2 = (bf16[512,512]{1,0:T(8,128)(2,1)S(1)}, bf16[512,512]{1,0:T(8,128)(2,1)}, u32[]{:S(2)}) copy-start(bf16[512,512]{1,0:T(8,128)(2,1)} %ck_hbm.1) | copy-start | bytes 1572868
  5.1 1.0 %copy-start.3 = (bf16[512,512]{1,0:T(8,128)(2,1)S(1)}, bf16[512,512]{1,0:T(8,128)(2,1)}, u32[]{:S(2)}) copy-start(bf16[512,512]{1,0:T(8,128)(2,1)} %cv_hbm.1) | copy-start | bytes 1572868
  6.1 0.8 %copy-start.6 = (bf16[4,4096]{1,0:T(4,128)(2,1)S(1)}, bf16[4,4096]{1,0:T(4,128)(2,1)}, u32[]{:S(2)}) copy-start(bf16[4,4096]{1,0:T(4,128)(2,1)} %hq.1) | copy-start | bytes 98308
  6.9 0.7 %copy-start.7 = (bf16[4,512]{1,0:T(4,128)(2,1)S(1)}, bf16[4,512]{1,0:T(4,128)(2,1)}, u32[]{:S(2)}) copy-start(bf16[4,512]{1,0:T(4,128)(2,1)} %hk.1) | copy-start | bytes 12292
  7.5 0.7 %copy-start.8 = (bf16[4,512]{1,0:T(4,128)(2,1)S(1)}, bf16[4,512]{1,0:T(4,128)(2,1)}, u32[]{:S(2)}) copy-start(bf16[4,512]{1,0:T(4,128)(2,1)} %hv.1) | copy-start | bytes 12292
  8.2 0.7 %copy-start.10 = (s32[32]{0:T(128)S(1)}, s32[32]{0:T(128)}, u32[]{:S(2)}) copy-start(s32[32]{0:T(128)} %param.17) | copy-start | bytes 388
  8.9 0.7 %copy-start.11 = (s32[32]{0:T(128)S(1)}, s32[32]{0:T(128)}, u32[]{:S(2)}) copy-start(s32[32]{0:T(128)} %param.18) | copy-start | bytes 388
  9.5 30.6 %copy-start.1 = (bf16[448,4096]{1,0:T(8,128)(2,1)S(1)}, bf16[448,4096]{1,0:T(8,128)(2,1)}, u32[]{:S(2)}) copy-start(bf16[448,4096]{1,0:T(8,128)(2,1)} %q_ref.1) | copy-start | bytes 11010052
  9.5 30.6 %copy-start.4 = (bf16[448,512]{1,0:T(8,128)(2,1)S(1)}, bf16[448,512]{1,0:T(8,128)(2,1)}, u32[]{:S(2)}) copy-start(bf16[448,512]{1,0:T(8,128)(2,1)} %k_ref.1) | copy-start | bytes 1376260
  9.6 30.6 %copy-start.5 = (bf16[448,512]{1,0:T(8,128)(2,1)S(1)}, bf16[448,512]{1,0:T(8,128)(2,1)}, u32[]{:S(2)}) copy-start(bf16[448,512]{1,0:T(8,128)(2,1)} %v_ref.1) | copy-start | bytes 1376260
  9.6 30.6 %copy-start.9 = (s32[1,448]{1,0:T(1,128)S(1)}, s32[1,448]{1,0:T(1,128)}, u32[]{:S(2)}) copy-start(s32[1,448]{1,0:T(1,128)} %doc_ref.1) | copy-start | bytes 5380

commit v2 on v1

--- a/solution.py
+++ b/solution.py
@@ -12,6 +12,7 @@
 LANES = 128
 ROW_BLOCK = 32
 MASKED = -1e30
+SHARES = (0.0, 0.3, 0.45, 0.8, 0.92, 1.0)
 SCALE = HEAD_DIM ** (-0.5)
 F32 = jnp.float32
 BF16 = jnp.bfloat16
@@ -42,59 +43,27 @@
         bias_ref[first : first + ROW_BLOCK, :span] = jnp.where(allowed, 0.0, MASKED)
 
 
-def prompt_group(query, key, value, bias_ref, wide_ref, out, group_size):
+def prompt_blocks(query, key, value, bias_ref, wide_ref, out, group_size, head_group, blocks):
     rows = key.shape[0]
-    wide_ref[:, :HEAD_DIM] = value[...]
+    lanes = slice(head_group * HEAD_DIM, (head_group + 1) * HEAD_DIM)
+    base = head_group * group_size * HEAD_DIM
     factor = SCALE * math.log2(math.e)
-    for first, low, high in windows(rows)[1]:
+    for first, low, high in blocks:
+        if first == 0:
+            wide_ref[:, :HEAD_DIM] = value[:, lanes]
         span = high - low
         block = slice(first, first + ROW_BLOCK)
-        stacked = jnp.concatenate(
-            [query[block, h * HEAD_DIM : (h + 1) * HEAD_DIM] for h in range(group_size)], axis=0
-        )
-        scores = lax.dot_general(stacked, key[low:high, :], NT, preferred_element_type=F32)
+        heads = [slice(base + h * HEAD_DIM, base + (h + 1) * HEAD_DIM) for h in range(group_size)]
+        stacked = jnp.concatenate([query[block, head] for head in heads], axis=0)
+        scores = lax.dot_general(stacked, key[low:high, lanes], NT, preferred_element_type=F32)
         scores = scores.reshape(group_size, ROW_BLOCK, span) + bias_ref[block, :span][None]
         highest = jnp.max(scores, axis=-1, keepdims=True)
         weights = jnp.exp2((scores - highest) * factor).astype(BF16)
         weights = weights.reshape(group_size * ROW_BLOCK, span)
         result = jnp.dot(weights, wide_ref[low:high, :], preferred_element_type=F32)
         result = (result[:, :HEAD_DIM] / result[:, HEAD_DIM:]).astype(BF16)
-        for h in range(group_size):
-            out[block, h * HEAD_DIM : (h + 1) * HEAD_DIM] = result[
-                h * ROW_BLOCK : (h + 1) * ROW_BLOCK
-            ]
-
-
-def prompt_kernel(group_size, doc_ref, q_ref, k_ref, v_ref, o_ref, bias_ref, wide_ref):
-    @pl.when(pl.program_id(0) == 0)
-    def _():
-        fill_bias(doc_ref, bias_ref)
-        wide_ref[:, HEAD_DIM:] = jnp.ones((wide_ref.shape[0], HEAD_DIM), BF16)
-
-    prompt_group(q_ref, k_ref, v_ref, bias_ref, wide_ref, o_ref, group_size)
-
-
-def prompt_attention(prompt_query, prompt_key, prompt_value, doc_ids):
-    rows = prompt_query.shape[0]
-    kv_local = prompt_key.shape[1] // HEAD_DIM
-    width = prompt_query.shape[1] // kv_local
-    return pl.pallas_call(
-        functools.partial(prompt_kernel, width // HEAD_DIM),
-        grid=(kv_local,),
-        out_shape=jax.ShapeDtypeStruct(prompt_query.shape, BF16),
-        in_specs=[
-            pl.BlockSpec((1, rows), lambda g: (0, 0)),
-            pl.BlockSpec((rows, width), lambda g: (0, g)),
-            pl.BlockSpec((rows, HEAD_DIM), lambda g: (0, g)),
-            pl.BlockSpec((rows, HEAD_DIM), lambda g: (0, g)),
-        ],
-        out_specs=pl.BlockSpec((rows, width), lambda g: (0, g)),
-        scratch_shapes=[
-            pltpu.VMEM((rows, windows(rows)[0]), F32),
-            pltpu.VMEM((rows, 2 * HEAD_DIM), BF16),
-        ],
-        compiler_params=pltpu.CompilerParams(vmem_limit_bytes=40 * 1024 * 1024),
-    )(doc_ids, prompt_query, prompt_key, prompt_value)
+        for h, head in enumerate(heads):
+            out[block, head] = result[h * ROW_BLOCK : (h + 1) * ROW_BLOCK]
 
 
 def routing(start_row, len_row, me, cap_rows, n, slots):
@@ -126,24 +95,59 @@
     return jnp.dot(select, flat[:, :width].astype(BF16), preferred_element_type=F32)
 
 
-def decode_kernel(
-    n, tps, start_ref, len_ref, hq, hk, hv, ck_hbm, cv_hbm, w_hbm, out_ref,
+def spread(buffers, mine, direct, relay, me, n):
+    partner = me + 1 - 2 * lax.rem(me, 2)
+    firsts, relays = [], []
+    for d in range(n // 2):
+        peer = partner if d == 0 else lax.rem(me + 2 * d, n)
+        origin = lax.rem(me - 2 * d + n, n)
+        for i, (buffer, block) in enumerate(zip(buffers, mine)):
+            firsts.append(
+                pltpu.make_async_remote_copy(
+                    src_ref=block, dst_ref=buffer.at[me],
+                    send_sem=direct.at[0, i, d], recv_sem=direct.at[1, i, d],
+                    device_id={"pool": peer}, device_id_type=MESH,
+                )
+            )
+            if d > 0:
+                relays.append(
+                    pltpu.make_async_remote_copy(
+                        src_ref=buffer.at[origin], dst_ref=buffer.at[origin],
+                        send_sem=relay.at[0, i, d], recv_sem=relay.at[1, i, d],
+                        device_id={"pool": partner}, device_id_type=MESH,
+                    )
+                )
+    return firsts, relays
+
+
+def start_relays(firsts, relays):
+    skip = len(firsts) - len(relays)
+    for first, relay in zip(firsts[skip:], relays):
+        first.wait_recv()
+        relay.start()
+
+
+def step_kernel(
+    n, tps, shares, start_ref, len_ref, doc_ref, hq, hk, hv, ck_hbm, cv_hbm, w_hbm,
+    pq_hbm, pk_hbm, pv_hbm, out_ref, prompt_ref,
     all_q, all_k, all_v, flat, ck, cv, w, pooled, part, part_in,
-    load_sem, w_sem, send_sem, recv_sem, out_send, out_recv, tp_send, tp_recv,
+    pq, pk, pv, prompt_out, bias_ref, wide_ref,
+    load_sem, w_sem, pq_sem, store_sem, direct_sem, relay_sem, out_direct, out_relay,
+    tp_send, tp_recv,
 ):
     me, tpi = lax.axis_index("pool"), lax.axis_index("tp")
     slots = pooled.shape[1]
     cap_rows = ck.shape[0]
     kv_local = ck.shape[1] // HEAD_DIM
     group_size = hq.shape[1] // ck.shape[1]
+    group_width = group_size * HEAD_DIM
     pieces = w_sem.shape[0]
     depth = w.shape[0] // pieces
 
     barrier = pltpu.get_barrier_semaphore()
-    for d in range(1, n):
-        pl.semaphore_signal(
-            barrier, inc=1, device_id={"pool": lax.rem(me + d, n)}, device_id_type=MESH
-        )
+    for d in range(n // 2):
+        peer = me + 1 - 2 * lax.rem(me, 2) if d == 0 else lax.rem(me + 2 * d, n)
+        pl.semaphore_signal(barrier, inc=1, device_id={"pool": peer}, device_id_type=MESH)
     for d in range(1, tps):
         pl.semaphore_signal(
             barrier, inc=1, device_id={"tp": lax.rem(tpi + d, tps)}, device_id_type=MESH
@@ -151,41 +155,64 @@
     loads = [
         pltpu.make_async_copy(src, dst, load_sem.at[i])
         for i, (src, dst) in enumerate(
-            [(hq, all_q.at[me]), (hk, all_k.at[me]), (hv, all_v.at[me]), (ck_hbm, ck), (cv_hbm, cv)]
+            [
+                (pk_hbm, pk), (pv_hbm, pv), (hq, all_q.at[me]), (hk, all_k.at[me]),
+                (hv, all_v.at[me]), (ck_hbm, ck), (cv_hbm, cv),
+            ]
         )
     ]
-    for load in loads:
-        load.start()
+    groups = [slice(g * group_width, (g + 1) * group_width) for g in range(kv_local)]
+    pq_loads = [
+        pltpu.make_async_copy(pq_hbm.at[:, span], pq.at[:, span], pq_sem.at[g])
+        for g, span in enumerate(groups)
+    ]
+    stores = [
+        pltpu.make_async_copy(prompt_out.at[:, span], prompt_ref.at[:, span], store_sem.at[g])
+        for g, span in enumerate(groups)
+    ]
     w_loads = [
         pltpu.make_async_copy(
             w_hbm.at[i * depth : (i + 1) * depth], w.at[i * depth : (i + 1) * depth], w_sem.at[i]
         )
         for i in range(pieces)
     ]
-    for load in w_loads:
+    for load in loads[:2] + pq_loads[:1] + loads[2:] + pq_loads[1:] + w_loads:
         load.start()
-    pl.semaphore_wait(barrier, n - 1 + tps - 1)
-    sends = []
-    for d in range(1, n):
-        for i, (src, dst) in enumerate([(hq, all_q), (hk, all_k), (hv, all_v)]):
-            sends.append(
-                pltpu.make_async_remote_copy(
-                    src_ref=src, dst_ref=dst.at[me],
-                    send_sem=send_sem.at[i, d], recv_sem=recv_sem.at[i, d],
-                    device_id={"pool": lax.rem(me + d, n)}, device_id_type=MESH,
-                )
+
+    blocks = windows(pk.shape[0])[1]
+    work = [(g, block) for g in range(kv_local) for block in blocks]
+
+    def prompt_share(share):
+        low, high = (round(len(work) * shares[share + k]) for k in range(2))
+        for g, block in work[low:high]:
+            if block is blocks[0]:
+                pq_loads[g].wait()
+            prompt_blocks(
+                pq, pk, pv, bias_ref, wide_ref, prompt_out, group_size, g, [block]
             )
-            sends[-1].start()
-
+            if block is blocks[-1]:
+                stores[g].start()
+
+    pl.semaphore_wait(barrier, n // 2 + tps - 1)
+    firsts, relays = spread(
+        (all_q, all_k, all_v), (hq, hk, hv), direct_sem, relay_sem, me, n
+    )
+    for copy in firsts:
+        copy.start()
+    fill_bias(doc_ref, bias_ref)
+    wide_ref[:, HEAD_DIM:] = jnp.ones((wide_ref.shape[0], HEAD_DIM), BF16)
+    for load in loads:
+        load.wait()
     select, first, length, unpack = routing(start_ref[...], len_ref[...], me, cap_rows, n, slots)
     at = lax.broadcasted_iota(jnp.int32, (slots, cap_rows), 1)
     bias = jnp.where((at >= first) & (at < first + length), 0.0, MASKED)
     bias = jnp.concatenate([bias] * group_size, axis=0)
 
-    for load in loads:
-        load.wait()
-    for send in sends:
-        send.wait()
+    prompt_share(0)
+    start_relays(firsts, relays)
+    prompt_share(1)
+    for copy in firsts[: len(firsts) - len(relays)] + relays:
+        copy.wait_recv()
     slot_key = slot_rows(select, all_k, flat)
     slot_value = slot_rows(select, all_v, flat)
     slot_query = slot_rows(select, all_q, flat)
@@ -219,20 +246,16 @@
                 h * slots : (h + 1) * slots
             ].astype(BF16)
 
-    sends = []
-    for d in range(1, n):
-        sends.append(
-            pltpu.make_async_remote_copy(
-                src_ref=pooled.at[me], dst_ref=pooled.at[me],
-                send_sem=out_send.at[d], recv_sem=out_recv.at[d],
-                device_id={"pool": lax.rem(me + d, n)}, device_id_type=MESH,
-            )
-        )
-        sends[-1].start()
+    out_firsts, out_relays = spread((pooled,), (pooled.at[me],), out_direct, out_relay, me, n)
+    for copy in out_firsts:
+        copy.start()
+    prompt_share(2)
+    start_relays(out_firsts, out_relays)
+    prompt_share(3)
     for load in w_loads:
         load.wait()
-    for send in sends:
-        send.wait()
+    for copy in out_firsts[: len(out_firsts) - len(out_relays)] + out_relays:
+        copy.wait_recv()
     sums = None
     for i in range(pieces):
         span = slice(i * depth, (i + 1) * depth)
@@ -254,30 +277,42 @@
             )
         )
         sends[-1].start()
+    prompt_share(4)
+    for copy in firsts + relays + out_firsts + out_relays:
+        copy.wait_send()
     for send in sends:
         send.wait()
     total = part[tpi]
     for d in range(1, tps):
         total = total + part_in[d]
     out_ref[...] = total.astype(BF16)
-
-
-def decode(
-    n, tps, home_query, home_key, home_value, cache_keys, cache_values, start, length, out_weight
+    for store in stores:
+        store.wait()
+
+
+def step(
+    n, tps, home_query, home_key, home_value, cache_keys, cache_values, start, length,
+    prompt_query, prompt_key, prompt_value, doc_ids, out_weight,
 ):
     requests = start.shape[0]
     home_rows, width = home_query.shape
     kv_width = home_key.shape[1]
+    kv_local = kv_width // HEAD_DIM
+    rows = prompt_query.shape[0]
     slots = 2 * home_rows
     out_rows, out_cols = requests // tps, out_weight.shape[1]
     pieces = 4
-    vmem, hbm = pl.BlockSpec(memory_space=pltpu.VMEM), pl.BlockSpec(memory_space=pl.ANY)
+    vmem, hbm = pl.BlockSpec(memory_space=pltpu.VMEM), pl.BlockSpec(memory_space=pltpu.HBM)
     dma = pltpu.SemaphoreType.DMA
-    return pl.pallas_call(
-        functools.partial(decode_kernel, n, tps),
-        out_shape=jax.ShapeDtypeStruct((out_rows, out_cols), BF16),
-        in_specs=[vmem, vmem] + [hbm] * 6,
-        out_specs=vmem,
+    half = n // 2
+    decode_out, prompt_out = pl.pallas_call(
+        functools.partial(step_kernel, n, tps, SHARES),
+        out_shape=[
+            jax.ShapeDtypeStruct((out_rows, out_cols), BF16),
+            jax.ShapeDtypeStruct(prompt_query.shape, BF16),
+        ],
+        in_specs=[vmem] * 3 + [hbm] * 9,
+        out_specs=[vmem, hbm],
         scratch_shapes=[
             pltpu.VMEM((n, home_rows, width), BF16),
             pltpu.VMEM((n, home_rows, kv_width), BF16),
@@ -289,16 +324,25 @@
             pltpu.VMEM((n, slots, width), BF16),
             pltpu.VMEM((tps, out_rows, out_cols), F32),
             pltpu.VMEM((tps, out_rows, out_cols), F32),
-            dma((5,)), dma((pieces,)), dma((3, n)), dma((3, n)),
-            dma((n,)), dma((n,)), dma((tps,)), dma((tps,)),
+            pltpu.VMEM(prompt_query.shape, BF16),
+            pltpu.VMEM(prompt_key.shape, BF16),
+            pltpu.VMEM(prompt_value.shape, BF16),
+            pltpu.VMEM(prompt_query.shape, BF16),
+            pltpu.VMEM((rows, windows(rows)[0]), F32),
+            pltpu.VMEM((rows, 2 * HEAD_DIM), BF16),
+            dma((7,)), dma((pieces,)), dma((kv_local,)), dma((kv_local,)),
+            dma((2, 3, half)), dma((2, 3, half)), dma((2, 1, half)), dma((2, 1, half)),
+            dma((tps,)), dma((tps,)),
         ],
         compiler_params=pltpu.CompilerParams(
-            collective_id=0, has_side_effects=True, vmem_limit_bytes=40 * 1024 * 1024
+            collective_id=0, has_side_effects=True, vmem_limit_bytes=60 * 1024 * 1024
         ),
     )(
-        start.reshape(1, requests), length.reshape(1, requests),
+        start.reshape(1, requests), length.reshape(1, requests), doc_ids,
         home_query, home_key, home_value, cache_keys, cache_values, out_weight,
+        prompt_query, prompt_key, prompt_value,
     )
+    return prompt_out, decode_out
 
 
 def solution(mesh):
@@ -308,12 +352,10 @@
         home_query, home_key, home_value, cache_keys, cache_values, cache_start, cache_len,
         prompt_query, prompt_key, prompt_value, doc_ids, out_weight,
     ):
-        decode_out = decode(
+        return step(
             n, tps, home_query, home_key, home_value, cache_keys, cache_values,
-            cache_start, cache_len, out_weight,
-        )
-        prompt_out = prompt_attention(prompt_query, prompt_key, prompt_value, doc_ids)
-        return prompt_out, decode_out
+            cache_start, cache_len, prompt_query, prompt_key, prompt_value, doc_ids, out_weight,
+        )
 
     return jax.shard_map(
         local,

time: 48.9 us -> 33.8 us (0.69)
  the two profiles are of different devices: /device:TPU:29 before, /device:TPU:0 now
where the time goes in v2:
time: 33.8 us; the launch traced here: 33.7 us
  Pallas kernels  28.1 us (83%)
  local copies, waits for them, and re-layouts  4.92 us (15%)
  between operations  0.65 us (2%)
    pallas_call x1, Pallas kernels, step(): pl.pallas_call(functools.partial(step_kernel, n, tps, SHARES), out_shape=...  28.1 us
    unnamed x4, local copies, waits for them, and re-layouts  4.92 us

profile of v2, /device:TPU:0, one launch (start us, length us, event | category | flops | bytes accessed | tf_op | source)
XLA Modules:
  0.0 33.7 jit_solution(14946852599382934251)
XLA Ops:
  0.6 28.1 %shard_map.131 = (bf16[16,1024]{1,0:T(8,128)(2,1)}, bf16[448,4096]{1,0:T(8,128)(2,1)}) custom-call(s32[1,32]{1,0:T(1,128)} %bitcast.2, s32[1,32]{1,0:T(1,128)} %bitcast.3, s32[1,448]{1,0:T(1,128)} %doc_ref.1, bf16[4,4096]{1,0:T(4,128)(2,1)} %hq.1, bf16[4,512]{1,0:T(4,128)(2,1)} %hk.1, bf16[4,512]{1,0:T(4,128)(2,1)} %hv.1, bf16[512,512]{1,0:T(8,128)(2,1)} %ck_hbm.1, ...), custom_call_target="tpu_custom_call" | custom-call | tf_op jit(solution)/shard_map/pallas_call | solution.py:308
  28.7 0.0 copy-start
  28.7 4.3 %copy.16 = bf16[448,4096]{1,0:T(8,128)(2,1)} copy(bf16[448,4096]{1,0:T(8,128)(2,1)} %get-tuple-element.8) | data formatting | bytes 7340032
  33.0 0.0 copy-done
  33.0 0.6 %copy.17 = bf16[16,1024]{1,0:T(8,128)(2,1)} copy(bf16[16,1024]{1,0:T(8,128)(2,1)S(1)} %copy-done) | data formatting | bytes 65536
Async XLA Ops:
  28.7 4.3 %copy-start = (bf16[16,1024]{1,0:T(8,128)(2,1)S(1)}, bf16[16,1024]{1,0:T(8,128)(2,1)}, u32[]{:S(2)}) copy-start(bf16[16,1024]{1,0:T(8,128)(2,1)} %get-tuple-element.9) | copy-start | bytes 98308
